TPU v7x, 256 devices: a whole 4x4x8 slice. The times are simulated.
256 devices in a mesh: row: 16 (over x, z_lo, core), col: 16 (over y, z_hi).
Axes of the slice: x: 4, y: 4, z: 8 (z_hi: 4, z_lo: 2; z = z_hi * 2 + z_lo), core: 2. Of those that a mesh axis runs over, the one named last changes fastest.
Arguments:
- source: float32 [262144, 256], P(('row', 'col')), may hold values from -6 to 6
- leaf_in: float32 [1024, 128, 256], P(('row', 'col')), may hold values from -0.375 to 0.375
- factors: float32 [10, 1024, 128, 256], P(None, ('row', 'col')), may hold values from -0.375 to 0.375
- leaf_out: float32 [1024, 256, 128], P(('row', 'col')), may hold values from -0.5 to 0.5
- weight_table: float32 [1024, 256], P(('row', 'col')), may hold values from 0.25 to 4
- block_index: int32 [1024], P(('row', 'col')), may hold values from 0 to 1023
Outputs:
- result: float32 [262144, 256], P(('row', 'col'))
All inputs are finite; a program needn't handle non-finite values.
Results may differ from a plain program's by a relative error of at most 0.0001.
Values sent between devices are 32-bit elements; how exact they have to be, the bound alone decides.
A program may use at most 64 MiB of HBM per device.

v0:
```python
import jax
import jax.numpy as jnp
from jax import lax
from jax.sharding import PartitionSpec as P

HIGH = lax.Precision.HIGHEST


def partner_2(value, axis, bit):
    return lax.ppermute(value, axis, [(i, i ^ 1 << bit) for i in range(lax.axis_size(axis))])


def local_partner(blocks, level_index):
    stride = 1 << level_index
    node_count = blocks.shape[0]
    shaped = blocks.reshape(node_count // (2 * stride), 2, stride, blocks.shape[1], blocks.shape[2])
    return shaped[:, ::-1].reshape(blocks.shape)


def partner(blocks, level_index, local_bits, col_bits):
    if level_index < local_bits:
        return local_partner(blocks, level_index)
    position = level_index - local_bits
    if position < col_bits:
        return partner_2(blocks, "col", position)
    return partner_2(blocks, "row", position - col_bits)


def body(source, leaf_in, factors, leaf_out, weight_table, block_index):
    level_count = factors.shape[0]
    node_count = leaf_in.shape[0]
    rank_size = leaf_in.shape[1]
    leaf_size = leaf_in.shape[2]
    column_count = source.shape[1]
    local_bits = node_count.bit_length() - 1
    col_bits = lax.axis_size("col").bit_length() - 1
    leaves = source.reshape(node_count, leaf_size, column_count)
    coefficients = jnp.einsum("nrk,nks->nrs", leaf_in, leaves, precision=HIGH)
    for level_index in range(level_count):
        received = partner(coefficients, level_index, local_bits, col_bits)
        stacked = jnp.concatenate([coefficients, received], axis=1)
        coefficients = jnp.einsum("nrk,nks->nrs", factors[level_index], stacked, precision=HIGH)
    image = jnp.einsum("nlr,nrs->nls", leaf_out, coefficients, precision=HIGH)
    piece = lax.all_gather(weight_table, ("row", "col"), axis=0, tiled=True)
    positions = lax.iota(jnp.int32, piece.shape[0])
    one_hot = (block_index[:, None] == positions[None, :]).astype(jnp.float32)
    profiles = jnp.dot(one_hot, piece, precision=HIGH)
    scaled = profiles[:, :, None] * image
    adjoint = jnp.einsum("nlr,nls->nrs", leaf_out, scaled, precision=HIGH)
    for level_index in reversed(range(level_count)):
        own_part = factors[level_index][:, :, :rank_size]
        cross_part = factors[level_index][:, :, rank_size:]
        own_cross = jnp.einsum("nrk,nrs->nks", cross_part, adjoint, precision=HIGH)
        cross_term = partner(own_cross, level_index, local_bits, col_bits)
        adjoint = jnp.einsum("nrk,nrs->nks", own_part, adjoint, precision=HIGH) + cross_term
    result = jnp.einsum("nrl,nrs->nls", leaf_in, adjoint, precision=HIGH)
    return result.reshape(node_count * leaf_size, column_count)


def solution(mesh):
    placed = (
        P(("row", "col"), None),
        P(("row", "col"), None, None),
        P(None, ("row", "col"), None, None),
        P(("row", "col"), None, None),
        P(("row", "col"), None),
        P(("row", "col")),
    )
    return jax.shard_map(
        body, mesh=mesh, in_specs=placed, out_specs=P(("row", "col"), None), check_vma=False
    )
```

profile of v0, /device:TPU:1, one launch (start us, length us, event | category | flops | bytes accessed | tf_op | source)
XLA Modules:
  0.0 799.6 jit_solution(3411981676963367168)
XLA Ops:
  9.6 1.8 fusion.10
  11.5 1.8 convolution_bitcast_fusion.25
  13.3 3.9 collective-permute-start
  17.2 22.3 %collective-permute-done = f32[4,128,256]{2,1,0:T(8,128)S(1)} collective-permute-done((f32[4,128,256]{2,1,0:T(8,128)S(1)}, f32[4,128,256]{2,1,0:T(8,128)S(1)}, u32[]{:S(2)}, u32[]{:S(2)}) %collective-permute-start) | collective-permute-done | bytes 524320 | tf_op jit(solution)/shard_map/ppermute | solution.py:10
  41.2 7.3 collective-permute-start.1
  48.5 22.7 %collective-permute-done.1 = f32[4,128,256]{2,1,0:T(8,128)S(1)} collective-permute-done((f32[4,128,256]{2,1,0:T(8,128)S(1)}, f32[4,128,256]{2,1,0:T(8,128)S(1)}, u32[]{:S(2)}, u32[]{:S(2)}) %collective-permute-start.1) | collective-permute-done | bytes 524320 | tf_op jit(solution)/shard_map/ppermute | solution.py:10
  71.2 1.8 convolution_bitcast_fusion.23
  74.4 10.6 %collective-permute-done.2 = f32[4,128,256]{2,1,0:T(8,128)S(1)} collective-permute-done((f32[4,128,256]{2,1,0:T(8,128)S(1)}, f32[4,128,256]{2,1,0:T(8,128)S(1)}, u32[]{:S(2)}, u32[]{:S(2)}) %collective-permute-start.2) | collective-permute-done | bytes 524320 | tf_op jit(solution)/shard_map/ppermute | solution.py:10
  85.0 1.8 convolution_bitcast_fusion.22
  86.8 3.0 collective-permute-start.3
  89.8 9.6 %collective-permute-done.3 = f32[4,128,256]{2,1,0:T(8,128)S(1)} collective-permute-done((f32[4,128,256]{2,1,0:T(8,128)S(1)}, f32[4,128,256]{2,1,0:T(8,128)S(1)}, u32[]{:S(2)}, u32[]{:S(2)}) %collective-permute-start.3) | collective-permute-done | bytes 524320 | tf_op jit(solution)/shard_map/ppermute | solution.py:10
  99.5 1.8 convolution_bitcast_fusion.21
  101.3 3.4 collective-permute-start.4
  108.1 13.1 %collective-permute-done.5 = f32[4,128,256]{2,1,0:T(8,128)S(1)} collective-permute-done((f32[4,128,256]{2,1,0:T(8,128)S(1)}, f32[4,128,256]{2,1,0:T(8,128)S(1)}, u32[]{:S(2)}, u32[]{:S(2)}) %collective-permute-start.5) | collective-permute-done | bytes 524320 | tf_op jit(solution)/shard_map/ppermute | solution.py:10
  124.5 11.2 %collective-permute-done.6 = f32[4,128,256]{2,1,0:T(8,128)S(1)} collective-permute-done((f32[4,128,256]{2,1,0:T(8,128)S(1)}, f32[4,128,256]{2,1,0:T(8,128)S(1)}, u32[]{:S(2)}, u32[]{:S(2)}) %collective-permute-start.6) | collective-permute-done | bytes 524320 | tf_op jit(solution)/shard_map/ppermute | solution.py:10
  135.7 2.6 convolution_bitcast_fusion.18
  138.3 2.7 collective-permute-start.7
  141.0 4.5 slice_bitcast_fusion.9
  145.5 496.2 %all-gather.3.cloned.1.call-done = f32[256,4,256]{2,1,0:T(4,128)} async-done(((f32[1,4,256]{2,1,0:T(4,128)}), f32[256,4,256]{2,1,0:T(4,128)}) %all-gather.3.cloned.1.call-update) | async-done | bytes 1048592 | tf_op jit(solution)/shard_map/all_gather | solution.py:44
  643.8 3.2 fusion.38
  647.0 2.1 convolution_multiply_fusion
  651.6 13.9 %collective-permute-done.8 = f32[4,128,256]{1,2,0:T(8,128)S(1)} collective-permute-done((f32[4,128,256]{1,2,0:T(8,128)S(1)}, f32[4,128,256]{1,2,0:T(8,128)S(1)}, u32[]{:S(2)}, u32[]{:S(2)}) %collective-permute-start.8) | collective-permute-done | bytes 524320 | tf_op jit(solution)/shard_map/ppermute | solution.py:10
  667.6 11.5 %collective-permute-done.9 = f32[4,128,256]{1,2,0:T(8,128)S(1)} collective-permute-done((f32[4,128,256]{1,2,0:T(8,128)S(1)}, f32[4,128,256]{1,2,0:T(8,128)S(1)}, u32[]{:S(2)}, u32[]{:S(2)}) %collective-permute-start.9) | collective-permute-done | bytes 524320 | tf_op jit(solution)/shard_map/ppermute | solution.py:10
  681.8 10.4 %collective-permute-done.10 = f32[4,128,256]{1,2,0:T(8,128)S(1)} collective-permute-done((f32[4,128,256]{1,2,0:T(8,128)S(1)}, f32[4,128,256]{1,2,0:T(8,128)S(1)}, u32[]{:S(2)}, u32[]{:S(2)}) %collective-permute-start.10) | collective-permute-done | bytes 524320 | tf_op jit(solution)/shard_map/ppermute | solution.py:10
  693.4 3.0 collective-permute-start.11
  699.3 14.6 %collective-permute-done.12 = f32[4,128,256]{1,2,0:T(8,128)S(1)} collective-permute-done((f32[4,128,256]{1,2,0:T(8,128)S(1)}, f32[4,128,256]{1,2,0:T(8,128)S(1)}, u32[]{:S(2)}, u32[]{:S(2)}) %collective-permute-start.12) | collective-permute-done | bytes 524320 | tf_op jit(solution)/shard_map/ppermute | solution.py:10
  715.2 12.2 %collective-permute-done.13 = f32[4,128,256]{1,2,0:T(8,128)S(1)} collective-permute-done((f32[4,128,256]{1,2,0:T(8,128)S(1)}, f32[4,128,256]{1,2,0:T(8,128)S(1)}, u32[]{:S(2)}, u32[]{:S(2)}) %collective-permute-start.13) | collective-permute-done | bytes 524320 | tf_op jit(solution)/shard_map/ppermute | solution.py:10
  728.7 5.6 collective-permute-start.14
  734.3 12.2 %collective-permute-done.14 = f32[4,128,256]{1,2,0:T(8,128)S(1)} collective-permute-done((f32[4,128,256]{1,2,0:T(8,128)S(1)}, f32[4,128,256]{1,2,0:T(8,128)S(1)}, u32[]{:S(2)}, u32[]{:S(2)}) %collective-permute-start.14) | collective-permute-done | bytes 524320 | tf_op jit(solution)/shard_map/ppermute | solution.py:10
  747.7 13.9 %collective-permute-start.15 = (f32[4,128,256]{1,2,0:T(8,128)S(1)}, f32[4,128,256]{1,2,0:T(8,128)S(1)}, u32[]{:S(2)}, u32[]{:S(2)}) collective-permute-start(f32[4,128,256]{1,2,0:T(8,128)S(1)} %convolution_bitcast_fusion.2), channel_id=1, source_target_pairs={{0,1},{1,0},{2,3},{3,2},{4,5},{5,4},{6,7},{7,6},{8,9},{9,8},{10,11... | collective-permute-start | bytes 1572872 | tf_op jit(solution)/shard_map/ppermute | solution.py:10
  761.6 22.9 %collective-permute-done.15 = f32[4,128,256]{1,2,0:T(8,128)S(1)} collective-permute-done((f32[4,128,256]{1,2,0:T(8,128)S(1)}, f32[4,128,256]{1,2,0:T(8,128)S(1)}, u32[]{:S(2)}, u32[]{:S(2)}) %collective-permute-start.15) | collective-permute-done | bytes 524320 | tf_op jit(solution)/shard_map/ppermute | solution.py:10
  789.7 3.0 fusion.78
  (67 shorter events, 35.0 us)
Async XLA Ops:
  6.5 1.2 copy-start
  6.5 635.1 %all-gather.3.cloned.1.call-start = ((), (), s32[]{:S(2)}) async-start(), calls=%async_computation | async-start | bytes 1052672 | tf_op jit(solution)/shard_map/all_gather | solution.py:44
  13.3 26.2 %collective-permute-start = (f32[4,128,256]{2,1,0:T(8,128)S(1)}, f32[4,128,256]{2,1,0:T(8,128)S(1)}, u32[]{:S(2)}, u32[]{:S(2)}) collective-permute-start(f32[4,128,256]{2,1,0:T(8,128)S(1)} %convolution_bitcast_fusion.25), channel_id=1, source_target_pairs={{0,1},{1,0},{2,3},{3,2},{4,5},{5,4},{6,7},{7,6},{8,9},{9,8},{10,11... | collective-permute-start | bytes 1572872 | tf_op jit(solution)/shard_map/ppermute | solution.py:10
  41.2 30.0 %collective-permute-start.1 = (f32[4,128,256]{2,1,0:T(8,128)S(1)}, f32[4,128,256]{2,1,0:T(8,128)S(1)}, u32[]{:S(2)}, u32[]{:S(2)}) collective-permute-start(f32[4,128,256]{2,1,0:T(8,128)S(1)} %convolution_bitcast_fusion.24), channel_id=1, source_target_pairs={{0,2},{1,3},{2,0},{3,1},{4,6},{5,7},{6,4},{7,5},{8,10},{9,11},{10,... | collective-permute-start | bytes 1572872 | tf_op jit(solution)/shard_map/ppermute | solution.py:10
  73.0 12.0 %collective-permute-start.2 = (f32[4,128,256]{2,1,0:T(8,128)S(1)}, f32[4,128,256]{2,1,0:T(8,128)S(1)}, u32[]{:S(2)}, u32[]{:S(2)}) collective-permute-start(f32[4,128,256]{2,1,0:T(8,128)S(1)} %convolution_bitcast_fusion.23), channel_id=1, source_target_pairs={{0,4},{1,5},{2,6},{3,7},{4,0},{5,1},{6,2},{7,3},{8,12},{9,13},{10,... | collective-permute-start | bytes 1572872 | tf_op jit(solution)/shard_map/ppermute | solution.py:10
  86.8 12.6 %collective-permute-start.3 = (f32[4,128,256]{2,1,0:T(8,128)S(1)}, f32[4,128,256]{2,1,0:T(8,128)S(1)}, u32[]{:S(2)}, u32[]{:S(2)}) collective-permute-start(f32[4,128,256]{2,1,0:T(8,128)S(1)} %convolution_bitcast_fusion.22), channel_id=1, source_target_pairs={{0,8},{1,9},{2,10},{3,11},{4,12},{5,13},{6,14},{7,15},{8,0},{9,1},... | collective-permute-start | bytes 1572872 | tf_op jit(solution)/shard_map/ppermute | solution.py:10
  101.3 4.9 collective-permute-start.4
  108.0 13.2 %collective-permute-start.5 = (f32[4,128,256]{2,1,0:T(8,128)S(1)}, f32[4,128,256]{2,1,0:T(8,128)S(1)}, u32[]{:S(2)}, u32[]{:S(2)}) collective-permute-start(f32[4,128,256]{2,1,0:T(8,128)S(1)} %convolution_bitcast_fusion.20), channel_id=1, source_target_pairs={{0,32},{16,48},{32,0},{48,16},{64,96},{80,112},{96,64},{112,80},{1... | collective-permute-start | bytes 1572872 | tf_op jit(solution)/shard_map/ppermute | solution.py:10
  123.0 12.6 %collective-permute-start.6 = (f32[4,128,256]{2,1,0:T(8,128)S(1)}, f32[4,128,256]{2,1,0:T(8,128)S(1)}, u32[]{:S(2)}, u32[]{:S(2)}) collective-permute-start(f32[4,128,256]{2,1,0:T(8,128)S(1)} %convolution_bitcast_fusion.19), channel_id=1, source_target_pairs={{0,64},{16,80},{32,96},{48,112},{64,0},{80,16},{96,32},{112,48},{1... | collective-permute-start | bytes 1572872 | tf_op jit(solution)/shard_map/ppermute | solution.py:10
  138.3 505.0 %copy-start.10 = (s32[4]{0:T(128)S(1)}, s32[4]{0:T(128)}, u32[]{:S(2)}) copy-start(s32[4]{0:T(128)} %param.11) | copy-start | bytes 52
  138.3 505.5 %collective-permute-start.7 = (f32[4,128,256]{2,1,0:T(8,128)}, f32[4,128,256]{2,1,0:T(8,128)}, u32[]{:S(2)}, u32[]{:S(2)}) collective-permute-start(f32[4,128,256]{2,1,0:T(8,128)} %convolution_bitcast_fusion.18), channel_id=1, source_target_pairs={{0,128},{16,144},{32,160},{48,176},{64,192},{80,208},{96,224},{112... | collective-permute-start | bytes 1572872 | tf_op jit(solution)/shard_map/ppermute | solution.py:10
  643.3 5.8 copy-start.9
  643.3 6.9 copy-start.8
  643.3 22.9 %copy-start.7 = (f32[4,128,256]{2,1,0:T(8,128)S(1)}, f32[4,128,256]{2,1,0:T(8,128)}, u32[]{:S(2)}) copy-start(f32[4,128,256]{2,1,0:T(8,128)} %get-tuple-element.14) | copy-start | bytes 1572868
  647.0 32.8 %copy-start.6 = (f32[4,128,256]{2,1,0:T(8,128)S(1)}, f32[4,128,256]{2,1,0:T(8,128)}, u32[]{:S(2)}) copy-start(f32[4,128,256]{2,1,0:T(8,128)} %get-tuple-element.6) | copy-start | bytes 1572868
  650.2 42.6 %copy-start.5 = (f32[4,128,256]{2,1,0:T(8,128)S(1)}, f32[4,128,256]{2,1,0:T(8,128)}, u32[]{:S(2)}) copy-start(f32[4,128,256]{2,1,0:T(8,128)} %get-tuple-element.7) | copy-start | bytes 1572868
  650.8 47.8 %copy-start.4 = (f32[4,128,256]{2,1,0:T(8,128)S(1)}, f32[4,128,256]{2,1,0:T(8,128)}, u32[]{:S(2)}) copy-start(f32[4,128,256]{2,1,0:T(8,128)} %get-tuple-element.8) | copy-start | bytes 1572868
  650.8 14.7 %collective-permute-start.8 = (f32[4,128,256]{1,2,0:T(8,128)S(1)}, f32[4,128,256]{1,2,0:T(8,128)S(1)}, u32[]{:S(2)}, u32[]{:S(2)}) collective-permute-start(f32[4,128,256]{1,2,0:T(8,128)S(1)} %convolution_bitcast_fusion.16), channel_id=1, source_target_pairs={{0,128},{16,144},{32,160},{48,176},{64,192},{80,208},{96,224},{112... | collective-permute-start | bytes 1572872 | tf_op jit(solution)/shard_map/ppermute | solution.py:10
  666.8 47.7 %copy-start.3 = (f32[4,128,256]{2,1,0:T(8,128)S(1)}, f32[4,128,256]{2,1,0:T(8,128)}, u32[]{:S(2)}) copy-start(f32[4,128,256]{2,1,0:T(8,128)} %get-tuple-element.9) | copy-start | bytes 1572868
  666.8 12.4 %collective-permute-start.9 = (f32[4,128,256]{1,2,0:T(8,128)S(1)}, f32[4,128,256]{1,2,0:T(8,128)S(1)}, u32[]{:S(2)}, u32[]{:S(2)}) collective-permute-start(f32[4,128,256]{1,2,0:T(8,128)S(1)} %convolution_bitcast_fusion.14), channel_id=1, source_target_pairs={{0,64},{16,80},{32,96},{48,112},{64,0},{80,16},{96,32},{112,48},{1... | collective-permute-start | bytes 1572872 | tf_op jit(solution)/shard_map/ppermute | solution.py:10
  680.4 47.7 %copy-start.2 = (f32[4,128,256]{2,1,0:T(8,128)S(1)}, f32[4,128,256]{2,1,0:T(8,128)}, u32[]{:S(2)}) copy-start(f32[4,128,256]{2,1,0:T(8,128)} %get-tuple-element.10) | copy-start | bytes 1572868
  680.4 11.7 %collective-permute-start.10 = (f32[4,128,256]{1,2,0:T(8,128)S(1)}, f32[4,128,256]{1,2,0:T(8,128)S(1)}, u32[]{:S(2)}, u32[]{:S(2)}) collective-permute-start(f32[4,128,256]{1,2,0:T(8,128)S(1)} %convolution_bitcast_fusion.12), channel_id=1, source_target_pairs={{0,32},{16,48},{32,0},{48,16},{64,96},{80,112},{96,64},{112,80},{1... | collective-permute-start | bytes 1572872 | tf_op jit(solution)/shard_map/ppermute | solution.py:10
  693.4 53.7 %copy-start.1 = (f32[4,128,256]{2,1,0:T(8,128)S(1)}, f32[4,128,256]{2,1,0:T(8,128)}, u32[]{:S(2)}) copy-start(f32[4,128,256]{2,1,0:T(8,128)} %get-tuple-element.11) | copy-start | bytes 1572868
  693.4 4.5 collective-permute-start.11
  699.2 14.7 %collective-permute-start.12 = (f32[4,128,256]{1,2,0:T(8,128)S(1)}, f32[4,128,256]{1,2,0:T(8,128)S(1)}, u32[]{:S(2)}, u32[]{:S(2)}) collective-permute-start(f32[4,128,256]{1,2,0:T(8,128)S(1)} %convolution_bitcast_fusion.8), channel_id=1, source_target_pairs={{0,8},{1,9},{2,10},{3,11},{4,12},{5,13},{6,14},{7,15},{8,0},{9,1},... | collective-permute-start | bytes 1572872 | tf_op jit(solution)/shard_map/ppermute | solution.py:10
  715.1 12.3 %collective-permute-start.13 = (f32[4,128,256]{1,2,0:T(8,128)S(1)}, f32[4,128,256]{1,2,0:T(8,128)S(1)}, u32[]{:S(2)}, u32[]{:S(2)}) collective-permute-start(f32[4,128,256]{1,2,0:T(8,128)S(1)} %convolution_bitcast_fusion.6), channel_id=1, source_target_pairs={{0,4},{1,5},{2,6},{3,7},{4,0},{5,1},{6,2},{7,3},{8,12},{9,13},{10,... | collective-permute-start | bytes 1572872 | tf_op jit(solution)/shard_map/ppermute | solution.py:10
  728.7 17.8 %collective-permute-start.14 = (f32[4,128,256]{1,2,0:T(8,128)S(1)}, f32[4,128,256]{1,2,0:T(8,128)S(1)}, u32[]{:S(2)}, u32[]{:S(2)}) collective-permute-start(f32[4,128,256]{1,2,0:T(8,128)S(1)} %convolution_bitcast_fusion.4), channel_id=1, source_target_pairs={{0,2},{1,3},{2,0},{3,1},{4,6},{5,7},{6,4},{7,5},{8,10},{9,11},{10,... | collective-permute-start | bytes 1572872 | tf_op jit(solution)/shard_map/ppermute | solution.py:10
  747.7 36.8 %collective-permute-start.15 = (f32[4,128,256]{1,2,0:T(8,128)S(1)}, f32[4,128,256]{1,2,0:T(8,128)S(1)}, u32[]{:S(2)}, u32[]{:S(2)}) collective-permute-start(f32[4,128,256]{1,2,0:T(8,128)S(1)} %convolution_bitcast_fusion.2), channel_id=1, source_target_pairs={{0,1},{1,0},{2,3},{3,2},{4,5},{5,4},{6,7},{7,6},{8,9},{9,8},{10,11... | collective-permute-start | bytes 1572872 | tf_op jit(solution)/shard_map/ppermute | solution.py:10
Sparse Core Ops, SparseCore 0:
  104.8 536.8 all-gather.2
where the time goes:
time: 800 us
  waiting for transfers between devices  686 us (86%)
  starting transfers between devices  48.9 us (6%)
  matrix products  41.8 us (5%)
  between operations  13.9 us (2%)
  local copies, waits for them, and re-layouts  8.52 us (1%)
    all_gather x1, waiting for transfers between devices, body(): piece = lax.all_gather(weight_table, ('row', 'col'), axis=0, tiled=True)  496 us
    ppermute x16, waiting for transfers between devices, partner_2(): lax.ppermute(value, axis, [(i, i ^ 1 << bit) for i in range(lax.axis_size...  190 us
    ppermute x16, starting transfers between devices, partner_2(): lax.ppermute(value, axis, [(i, i ^ 1 << bit) for i in range(lax.axis_size...  48.9 us
    dot_general x10, matrix products, body(): jnp.einsum('nrk,nks->nrs', factors[level_index], stacked, precision=HIGH)  20.2 us
  transfers between devices with their start and end apart: 17, of which 16 were waited for; matrix products, arithmetic and copies ran while one was open for 2% of the time, Pallas kernels for 0%

commit v1 on v0

v1 whole, which is shorter than its diff:
```python
import functools

import jax
import jax.numpy as jnp
from jax import lax
from jax.experimental import pallas as pl
from jax.experimental.pallas import tpu as pltpu
from jax.sharding import PartitionSpec as P

MESH = pl.DeviceIdType.MESH
F32, BF16 = jnp.float32, jnp.bfloat16

HOP = {2: 5.2, 3: 6.4, 4: 3.0, 5: 3.0, 6: 1.5, 7: 3.0, 8: 3.0, 9: 3.0}
INTERVAL = 5.0
LEAD = 3


def plan(levels):
    order = list(range(2, levels)) + list(range(levels - 1, 1, -1))
    at = [0.0]
    for level in order:
        at.append(at[-1] + HOP[level])
    delay = [int(t // INTERVAL) for t in at]
    inside = sorted(range(len(at)), key=lambda s: (at[s] % INTERVAL, -s))
    return order, delay, inside


def halves(value):
    high = value.astype(BF16)
    low = (value - high.astype(F32)).astype(BF16)
    return high, low


def stacked(value):
    return jnp.concatenate(halves(value), axis=0)


def nt(a, b):
    return lax.dot_general(a, b, (((1,), (1,)), ((), ())), preferred_element_type=F32)


def nn(a, b):
    return lax.dot_general(a, b, (((1,), (0,)), ((), ())), preferred_element_type=F32)


def forward(state, factor):
    r = factor.shape[0] // 2
    c = state.shape[0]
    full = nt(stacked(state), factor)
    return (full[:c, :r] + full[:c, r:]) + (full[c:, :r] + full[c:, r:])


def backward(state, factor):
    c = state.shape[0]
    high, low = halves(state)
    left = jnp.concatenate(
        [jnp.concatenate([high, high], axis=1), jnp.concatenate([low, low], axis=1)], axis=0
    )
    full = nn(left, factor)
    return full[:c] + full[c:]


def flip(value, bit):
    step = 1 << bit
    return value + step - 2 * step * lax.rem(lax.div(value, step), 2)


def kernel(
    levels, col_bits, row_bits,
    index_ref, source_ref, leaf_in_ref, factors_ref, leaf_out_ref, table_ref, result_ref,
    src_v, lin_v, lout_v, fac_v, fb_v, linb_v, gram_v, tab_v, send_v, recv_v, own_v, loc_v, out_v,
    send_sem, recv_sem, tsend_sem, trecv_sem, fac_sem, src_sem, lin_sem, lout_sem, tab_sem, out_sem,
):
    nodes = 4
    chunks = 8
    rank = 128
    row, col = lax.axis_index("row"), lax.axis_index("col")
    device = row * (1 << col_bits) + col
    order, delay, inside = plan(levels)
    exchanges = len(order)
    half_way = exchanges // 2

    def partner(level):
        bit = level - 2
        if bit < col_bits:
            return (row, flip(col, bit))
        return (flip(row, bit - col_bits), col)

    def load_source(n):
        return pltpu.make_async_copy(source_ref.at[pl.ds(n * 256, 256)], src_v.at[n], src_sem.at[n])

    def load_leaf_in(n):
        return pltpu.make_async_copy(leaf_in_ref.at[n], lin_v.at[n], lin_sem.at[n])

    def load_factor(level, n):
        return pltpu.make_async_copy(factors_ref.at[level, n], fac_v.at[level, n], fac_sem.at[level, n])

    def load_leaf_out(n):
        return pltpu.make_async_copy(leaf_out_ref.at[n], lout_v.at[n], lout_sem.at[n])

    def load_table(n):
        return pltpu.make_async_copy(table_ref.at[pl.ds(n, 1)], tab_v.at[device * 4 + n], tab_sem.at[n])

    for n in range(nodes):
        load_table(n).start()
    for n in range(nodes):
        load_leaf_in(n).start()
        load_source(n).start()
    for level in range(levels):
        for n in range(nodes):
            load_factor(level, n).start()
    for n in range(nodes):
        load_leaf_out(n).start()

    barrier = pltpu.get_barrier_semaphore()
    for level in range(2, levels):
        pl.semaphore_signal(barrier, inc=1, device_id=partner(level), device_id_type=MESH)
    pl.semaphore_wait(barrier, levels - 2)

    def exchange(e, c):
        return pltpu.make_async_remote_copy(
            src_ref=send_v.at[e, c],
            dst_ref=recv_v.at[e, c],
            send_sem=send_sem.at[e, c],
            recv_sem=recv_sem.at[e, c],
            device_id=partner(order[e]),
            device_id_type=MESH,
        )

    def gather(k):
        size = 4 << k
        start = lax.div(device * 4, size) * size
        return pltpu.make_async_remote_copy(
            src_ref=tab_v.at[pl.ds(start, size)],
            dst_ref=tab_v.at[pl.ds(start, size)],
            send_sem=tsend_sem.at[k],
            recv_sem=trecv_sem.at[k],
            device_id=partner(k + 2),
            device_id_type=MESH,
        )

    def split_factor(level, n):
        load_factor(level, n).wait()
        fb_v[level, n] = stacked(fac_v[level, n])

    def start_leaf(h):
        for n in range(nodes):
            @pl.when(h == 0)
            def _():
                load_leaf_in(n).wait()
                load_source(n).wait()
                linb_v[n] = stacked(lin_v[n])
            x = src_v[n, :, pl.ds(pl.multiple_of(h * 128, 128), 128)]
            full = nn(linb_v[n], jnp.concatenate(halves(x), axis=1))
            coef = (full[:rank, :128] + full[:rank, 128:]) + (full[rank:, :128] + full[rank:, 128:])
            loc_v[0, n] = coef.T

    def start_level(level, h):
        for n in range(nodes):
            @pl.when(h == 0)
            def _():
                split_factor(level, n)
            other = n ^ (1 << level)
            new = forward(jnp.concatenate([loc_v[level, n], loc_v[level, other]], axis=1), fb_v[level, n])
            if level == 0:
                loc_v[1, n] = new
            else:
                send_v[0, h * 4 + n] = new

    def finish(n, h, state):
        both = backward(state, fb_v[1, n])
        loc_v[2, n] = both[:, :rank]
        loc_v[3, n] = both[:, rank:]

        for m in (0, 1):
            @pl.when(n == m + 2)
            def _():
                for q in (m, m + 2):
                    both = backward(loc_v[2, q] + loc_v[3, q ^ 2], fb_v[0, q])
                    loc_v[4, q] = both[:, :rank]
                    loc_v[5, q] = both[:, rank:]

        @pl.when(n == 3)
        def _():
            for q in range(nodes):
                block = backward(loc_v[4, q] + loc_v[5, q ^ 1], linb_v[q])
                out_v[h, q] = block.T
                store(h, q).start()

    def store(h, q):
        lanes = pl.ds(h * 128, 128) if isinstance(h, int) else pl.ds(pl.multiple_of(h * 128, 128), 128)
        return pltpu.make_async_copy(out_v.at[h, q], result_ref.at[pl.ds(q * 256, 256), lanes], out_sem.at[h, q])

    def make_gram(n):
        load_leaf_out(n).wait()
        leaf = lout_v[n]
        profile = tab_v[index_ref[n]]
        weighted = leaf.T * profile
        full = nn(stacked(weighted), jnp.concatenate(halves(leaf), axis=1))
        gram = (full[:rank, :rank] + full[:rank, rank:]) + (full[rank:, :rank] + full[rank:, rank:])
        gram_v[n] = stacked(gram)

    def step(s, c):
        n = lax.rem(c, 4)
        if s >= 1:
            exchange(s - 1, c).wait_recv()
        if s >= 2:
            exchange(s - 2, c).wait_send()
        if s == 0:
            exchange(0, c).start()
        elif s <= half_way:
            level = order[s - 1]

            @pl.when(c < 4)
            def _():
                split_factor(level, n)

            new = forward(jnp.concatenate([send_v[s - 1, c], recv_v[s - 1, c]], axis=1), fb_v[level, n])
            if s < half_way:
                send_v[s, c] = new
                exchange(s, c).start()
            else:
                @pl.when(c == 0)
                def _():
                    gather(levels - 3).wait_recv()

                @pl.when(c < 4)
                def _():
                    make_gram(n)

                both = backward(backward(new, gram_v[n]), fb_v[level, n])
                own_v[c] = both[:, :rank]
                send_v[s, c] = both[:, rank:]
                exchange(s, c).start()
        else:
            state = own_v[c] + recv_v[s - 1, c]
            if s < exchanges:
                level = order[s]
                both = backward(state, fb_v[level, n])
                own_v[c] = both[:, :rank]
                send_v[s, c] = both[:, rank:]
                exchange(s, c).start()
            else:
                finish(n, lax.div(c, 4), state)

    def iteration(i, carry):
        for first in (0, 4):
            @pl.when(i == first)
            def _():
                start_leaf(first // 4)

            @pl.when(i == first + 1)
            def _():
                start_level(0, first // 4)

            @pl.when(i == first + 2)
            def _():
                start_level(1, first // 4)
        for k in range(levels - 2):
            @pl.when(i == k)
            def _():
                if k == 0:
                    for n in range(nodes):
                        load_table(n).wait()
                else:
                    gather(k - 1).wait_recv()
                gather(k).start()
        for s in inside:
            c = i - (LEAD + delay[s])

            @pl.when(jnp.logical_and(c >= 0, c < chunks))
            def _():
                step(s, c)
        return carry

    lax.fori_loop(0, LEAD + chunks + max(delay), iteration, 0)

    def drain(c, carry):
        exchange(exchanges - 1, c).wait_send()
        return carry

    lax.fori_loop(0, chunks, drain, 0)
    for k in range(levels - 2):
        gather(k).wait_send()
    for h in range(2):
        for q in range(nodes):
            store(h, q).wait()


def body(source, leaf_in, factors, leaf_out, weight_table, block_index):
    levels = factors.shape[0]
    col_bits = lax.axis_size("col").bit_length() - 1
    row_bits = lax.axis_size("row").bit_length() - 1
    exchanges = 2 * (levels - 2)
    total = 4 << (levels - 2)
    anywhere = pl.BlockSpec(memory_space=pl.ANY)
    return pl.pallas_call(
        functools.partial(kernel, levels, col_bits, row_bits),
        out_shape=jax.ShapeDtypeStruct(source.shape, F32),
        in_specs=[pl.BlockSpec(memory_space=pltpu.SMEM)] + [anywhere] * 5,
        out_specs=anywhere,
        scratch_shapes=[
            pltpu.VMEM((4, 256, 256), F32),
            pltpu.VMEM((4, 128, 256), F32),
            pltpu.VMEM((4, 256, 128), F32),
            pltpu.VMEM((levels, 4, 128, 256), F32),
            pltpu.VMEM((levels, 4, 256, 256), BF16),
            pltpu.VMEM((4, 256, 256), BF16),
            pltpu.VMEM((4, 256, 128), BF16),
            pltpu.VMEM((total, 1, 256), F32),
            pltpu.VMEM((exchanges, 8, 128, 128), F32),
            pltpu.VMEM((exchanges, 8, 128, 128), F32),
            pltpu.VMEM((8, 128, 128), F32),
            pltpu.VMEM((6, 4, 128, 128), F32),
            pltpu.VMEM((2, 4, 256, 128), F32),
            pltpu.SemaphoreType.DMA((exchanges, 8)),
            pltpu.SemaphoreType.DMA((exchanges, 8)),
            pltpu.SemaphoreType.DMA((levels - 2,)),
            pltpu.SemaphoreType.DMA((levels - 2,)),
            pltpu.SemaphoreType.DMA((levels, 4)),
            pltpu.SemaphoreType.DMA((4,)),
            pltpu.SemaphoreType.DMA((4,)),
            pltpu.SemaphoreType.DMA((4,)),
            pltpu.SemaphoreType.DMA((4,)),
            pltpu.SemaphoreType.DMA((2, 4)),
        ],
        compiler_params=pltpu.CompilerParams(
            collective_id=0, has_side_effects=True, vmem_limit_bytes=60 << 20
        ),
        name="butterfly",
    )(block_index, source, leaf_in, factors, leaf_out, weight_table)


def solution(mesh):
    placed = (
        P(("row", "col"), None),
        P(("row", "col"), None, None),
        P(None, ("row", "col"), None, None),
        P(("row", "col"), None, None),
        P(("row", "col"), None),
        P(("row", "col")),
    )
    return jax.shard_map(
        body, mesh=mesh, in_specs=placed, out_specs=P(("row", "col"), None), check_vma=False
    )
```

time: 800 us -> 160 us (0.20)
  waiting for transfers between devices: 686 us -> 0 us
  Pallas kernels: 0 us -> 157 us
  starting transfers between devices: 48.9 us -> 0 us
  matrix products: 41.8 us -> 0 us
  between operations: 13.9 us -> 0.01 us
    all_gather x1 -> x0, waiting for transfers between devices: 496 us -> none  [body(): piece = lax.all_gather(weight_table, ('row', 'col'), axis=0, tiled=True)]
    ppermute x16 -> x0, waiting for transfers between devices: 190 us -> none  [partner_2(): lax.ppermute(value, axis, [(i, i ^ 1 << bit) for i in range(lax.axis_size...]
    pallas_call x0 -> x1, Pallas kernels: none -> 157 us  [body(): pl.pallas_call(functools.partial(kernel, levels, col_bits, row_bits), out...]
    ppermute x16 -> x0, starting transfers between devices: 48.9 us -> none  [partner_2(): lax.ppermute(value, axis, [(i, i ^ 1 << bit) for i in range(lax.axis_size...]
    dot_general x35 -> x0, matrix products: 41.8 us -> none  [the longest x10 20.2 us: body(): jnp.einsum('nrk,nks->nrs', factors[level_index], stacked, precision=HIGH)]
  transfers between devices with their start and end apart: 17 -> 0, of which waited for: 16 -> 0; matrix products, arithmetic and copies ran while one was open for 2% -> 0% of each run, Pallas kernels for 0% -> 0%
where the time goes in v1:
time: 160 us; the launch traced here: 159 us
  Pallas kernels  157 us (98%)
  local copies, waits for them, and re-layouts  2.26 us (1%)
    pallas_call x1, Pallas kernels, body(): pl.pallas_call(functools.partial(kernel, levels, col_bits, row_bits), out...  157 us

profile of v1, /device:TPU:1, one launch (start us, length us, event | category | flops | bytes accessed | tf_op | source)
XLA Modules:
  0.0 159.2 jit_solution(6584515655597552537)
XLA Ops:
  0.0 156.9 %butterfly.1 = f32[1024,256]{1,0:T(8,128)} custom-call(s32[4]{0:T(128)} %index_ref.1, f32[1024,256]{1,0:T(8,128)} %source_ref.1, f32[4,128,256]{2,1,0:T(8,128)} %leaf_in_ref.1, f32[10,4,128,256]{3,2,1,0:T(8,128)} %factors_ref.1, f32[4,256,128]{2,1,0:T(8,128)} %leaf_out_ref.1, f32[4,256]{1,0:T(4,128)} %table_ref.1), custom_call_target="tpu_custom_call" | custom-call | tf_op jit(solution)/shard_map/butterfly/pallas_call | solution.py:297
  156.9 2.3 %copy.8 = f32[1024,256]{1,0:T(8,128)} copy(f32[1024,256]{1,0:T(8,128)} %butterfly.1) | data formatting | bytes 2097152

commit v2 on v0

v2 whole, which is shorter than its diff:
```python
import functools

import jax
import jax.numpy as jnp
from jax import lax
from jax.experimental import pallas as pl
from jax.experimental.pallas import tpu as pltpu
from jax.sharding import PartitionSpec as P

MESH = pl.DeviceIdType.MESH
F32, BF16 = jnp.float32, jnp.bfloat16
NODES, RANK = 4, 128
WIDE = 64
CHUNKS = 256 // WIDE * NODES

HOP = {2: 5.0, 3: 6.2, 4: 3.0, 5: 3.6, 6: 1.8, 7: 3.2, 8: 3.0, 9: 3.8}
INTERVAL = 2.6
SECOND_AT = 9.0
GATHER = ((0, 1, 5), (2, 3), (6, 7), (4,))
GATHER_AT = (0.1, 10.0, 19.0, 31.0)
GRAM_AT = 38.0


def plan(levels):
    order = list(range(2, levels)) + list(range(levels - 1, 1, -1))
    at = [0.0]
    for level in order:
        at.append(at[-1] + HOP[level])
    steps = len(order) + 1
    events = [(c * INTERVAL + at[s], -s, s * CHUNKS + c) for s in range(steps) for c in range(CHUNKS)]
    events.append((SECOND_AT, 2, -1))
    base = steps * CHUNKS
    gram_at = min(GRAM_AT, at[len(order) // 2] - 0.01)
    rounds = len(gather_rounds(levels - 2))
    for k in range(rounds):
        events.append((min(GATHER_AT[k], gram_at - 0.1 + 0.01 * k), 1, base + k))
    for n in range(NODES):
        events.append((gram_at + n * INTERVAL, 1, base + rounds + n))
    return [code for _, _, code in sorted(events)]


def gather_rounds(bits):
    rounds, done = [], 0
    for group in GATHER:
        group = [b for b in group if b < bits]
        if group:
            masks = [sum(1 << b for i, b in enumerate(group) if m >> i & 1) for m in range(1, 1 << len(group))]
            rounds.append((done, masks))
            done += len(group)
    return rounds


def halves(value):
    high = value.astype(BF16)
    low = (value - high.astype(F32)).astype(BF16)
    return high, low


def stacked(value):
    return jnp.concatenate(halves(value), axis=0)


def nt(a, b):
    return lax.dot_general(a, b, (((1,), (1,)), ((), ())), preferred_element_type=F32)


def nn(a, b):
    return lax.dot_general(a, b, (((1,), (0,)), ((), ())), preferred_element_type=F32)


def quarters(full):
    m, k = full.shape[0] // 2, full.shape[1] // 2
    return (full[:m, :k] + full[:m, k:]) + (full[m:, :k] + full[m:, k:])


def forward(state, factor):
    return quarters(nt(stacked(state), factor))


def backward(state, factor):
    c = state.shape[0]
    high, low = halves(state)
    left = jnp.concatenate(
        [jnp.concatenate([high, high], axis=1), jnp.concatenate([low, low], axis=1)], axis=0
    )
    full = nn(left, factor)
    return full[:c] + full[c:]


def flip(value, bit):
    step = 1 << bit
    return value + step - 2 * step * lax.rem(lax.div(value, step), 2)


def kernel(
    levels, col_bits,
    index_ref, source_ref, leaf_in_ref, factors_ref, leaf_out_ref, table_ref, result_ref,
    src_v, lin_v, lout_v, fac_v, fb_v, linb_v, gram_v, tab_v, send_v, recv_v, own_v, loc_v, out_v,
    send_sem, recv_sem, tsend_sem, trecv_sem, fac_sem, src_sem, lin_sem, lout_sem, tab_sem, out_sem,
):
    bits = levels - 2
    cols = 1 << col_bits
    row, col = lax.axis_index("row"), lax.axis_index("col")
    device = row * cols + col
    exchanges = 2 * bits
    events = plan(levels)
    gather_bits = [b for group in GATHER for b in group if b < bits]
    rounds = gather_rounds(bits)

    def place(index):
        spot = 0
        for k, b in enumerate(gather_bits):
            spot = spot + lax.rem(lax.div(index, 1 << b), 2) * (1 << k)
        return spot

    def load_source(h, n):
        return pltpu.make_async_copy(
            source_ref.at[pl.ds(n * 256, 256), pl.ds(h * 128, 128)], src_v.at[h, n], src_sem.at[h, n]
        )

    def load_leaf_in(n):
        return pltpu.make_async_copy(leaf_in_ref.at[n], lin_v.at[n], lin_sem.at[n])

    def load_factor(level, n):
        return pltpu.make_async_copy(factors_ref.at[level, n], fac_v.at[level, n], fac_sem.at[level, n])

    def load_leaf_out(n):
        return pltpu.make_async_copy(leaf_out_ref.at[n], lout_v.at[n], lout_sem.at[n])

    mine = place(device)

    def load_table(n):
        return pltpu.make_async_copy(table_ref.at[pl.ds(n, 1)], tab_v.at[mine * NODES + n], tab_sem.at[n])

    def mate(mask):
        other = device
        for b in range(bits):
            if mask >> b & 1:
                other = flip(other, b)
        return (lax.div(other, cols), lax.rem(other, cols))

    barrier = pltpu.get_barrier_semaphore()
    mates = sorted({1 << b for b in range(bits)} | {mask for _, masks in rounds for mask in masks})
    for mask in mates:
        pl.semaphore_signal(barrier, inc=1, device_id=mate(mask), device_id_type=MESH)

    for n in range(NODES):
        load_leaf_in(n).start()
        load_source(0, n).start()
    for level in range(2):
        for n in range(NODES):
            load_factor(level, n).start()
    for n in range(NODES):
        load_table(n).start()

    def exchange(e, slot):
        b = e if e < bits else exchanges - 1 - e
        return pltpu.make_async_remote_copy(
            src_ref=send_v.at[slot],
            dst_ref=recv_v.at[slot],
            send_sem=send_sem.at[slot],
            recv_sem=recv_sem.at[slot],
            device_id=mate(1 << b),
            device_id_type=MESH,
        )

    def gather(k):
        done, masks = rounds[k]
        size = 1 << done
        rows = pl.ds(lax.div(mine, size) * size * NODES, size * NODES)
        return [
            pltpu.make_async_remote_copy(
                src_ref=tab_v.at[rows],
                dst_ref=tab_v.at[rows],
                send_sem=tsend_sem.at[mates.index(mask)],
                recv_sem=trecv_sem.at[mates.index(mask)],
                device_id=mate(mask),
                device_id_type=MESH,
            )
            for mask in masks
        ]

    def split_factor(level, n):
        load_factor(level, n).wait()
        fb_v[level, n] = stacked(fac_v[level, n])

    def store(h, q):
        lanes = pl.ds(h * 128, 128)
        return pltpu.make_async_copy(out_v.at[h, q], result_ref.at[pl.ds(q * 256, 256), lanes], out_sem.at[h, q])

    def start_half(h):
        for n in range(NODES):
            if h == 0:
                load_leaf_in(n).wait()
                linb_v[n] = stacked(lin_v[n])
            load_source(h, n).wait()
            loc_v[0, n] = quarters(nn(linb_v[n], jnp.concatenate(halves(src_v[h, n]), axis=1))).T
        for level in range(2):
            if h == 0:
                for n in range(NODES):
                    split_factor(level, n)
            for n in range(NODES):
                both = jnp.concatenate([loc_v[level, n], loc_v[level, n ^ (1 << level)]], axis=1)
                new = forward(both, fb_v[level, n])
                if level == 0:
                    loc_v[1, n] = new
                else:
                    for q in range(128 // WIDE):
                        send_v[(h * (128 // WIDE) + q) * NODES + n] = new[q * WIDE : (q + 1) * WIDE]

    def finish(c, state):
        n, q = c % NODES, c // NODES
        h, part = q * WIDE // 128, q % (128 // WIDE)
        rows = slice(part * WIDE, (part + 1) * WIDE)
        both = backward(state, fb_v[1, n])
        loc_v[2, n, rows] = both[:, :RANK]
        loc_v[3, n, rows] = both[:, RANK:]
        if n >= 2:
            for m in (n - 2, n):
                both = backward(loc_v[2, m, rows] + loc_v[3, m ^ 2, rows], fb_v[0, m])
                loc_v[4, m, rows] = both[:, :RANK]
                loc_v[5, m, rows] = both[:, RANK:]
        if n == 3 and rows.stop == 128:
            for m in range(NODES):
                block = backward(loc_v[4, m] + loc_v[5, m ^ 1], linb_v[m])
                out_v[h, m] = block.T
                store(h, m).start()

    def make_gram(n):
        load_leaf_out(n).wait()
        leaf = lout_v[n]
        index = index_ref[n]
        profile = tab_v[place(lax.div(index, NODES)) * NODES + lax.rem(index, NODES)]
        gram = quarters(nn(stacked(leaf.T * profile), jnp.concatenate(halves(leaf), axis=1)))
        gram_v[n] = stacked(gram)

    start_half(0)
    for n in range(NODES):
        load_factor(2, n).start()
        load_source(1, n).start()
    for level in range(3, levels):
        for n in range(NODES):
            load_factor(level, n).start()
    for n in range(NODES):
        load_leaf_out(n).start()
    for n in range(NODES):
        load_table(n).wait()
    pl.semaphore_wait(barrier, len(mates))

    def event(code):
        if code < 0:
            start_half(1)
            return
        s, c = code // CHUNKS, code % CHUNKS
        n, before = c % NODES, code - CHUNKS
        if s > exchanges:
            k = code - (exchanges + 1) * CHUNKS
            if 0 < k <= len(rounds):
                for copy in gather(k - 1):
                    copy.wait_recv()
            if k < len(rounds):
                for copy in gather(k):
                    copy.start()
            else:
                make_gram(k - len(rounds))
            return
        if s > 0:
            exchange(s - 1, before).wait_recv()
        if s < bits and s > 0:
            both = jnp.concatenate([send_v[before], recv_v[before]], axis=1)
            send_v[code] = forward(both, fb_v[s + 1, n])
        elif s == bits:
            both = jnp.concatenate([send_v[before], recv_v[before]], axis=1)
            new = forward(both, fb_v[levels - 1, n])
            both = backward(backward(new, gram_v[n]), fb_v[levels - 1, n])
            own_v[c] = both[:, :RANK]
            send_v[code] = both[:, RANK:]
        elif s > bits and s < exchanges:
            both = backward(own_v[c] + recv_v[before], fb_v[exchanges + 1 - s, n])
            own_v[c] = both[:, :RANK]
            send_v[code] = both[:, RANK:]
        if s < exchanges:
            exchange(s, code).start()
        else:
            finish(c, own_v[c] + recv_v[before])
        if s < bits and c < NODES:
            split_factor(s + 2, n)
        if s >= 2:
            exchange(s - 2, before - CHUNKS).wait_send()

    for code in events:
        event(code)

    def drain(c, carry):
        exchange(exchanges - 1, (exchanges - 1) * CHUNKS + c).wait_send()
        return carry

    lax.fori_loop(0, CHUNKS, drain, 0)
    for k in range(len(rounds)):
        for copy in gather(k):
            copy.wait_send()
    for h in range(2):
        for q in range(NODES):
            store(h, q).wait()


def body(source, leaf_in, factors, leaf_out, weight_table, block_index):
    levels = factors.shape[0]
    bits = levels - 2
    col_bits = lax.axis_size("col").bit_length() - 1
    slots = 2 * bits * CHUNKS
    mates = {1 << b for b in range(bits)} | {mask for _, masks in gather_rounds(bits) for mask in masks}
    anywhere = pl.BlockSpec(memory_space=pl.ANY)
    return pl.pallas_call(
        functools.partial(kernel, levels, col_bits),
        out_shape=jax.ShapeDtypeStruct(source.shape, F32),
        in_specs=[pl.BlockSpec(memory_space=pltpu.SMEM)] + [anywhere] * 5,
        out_specs=anywhere,
        scratch_shapes=[
            pltpu.VMEM((2, 4, 256, 128), F32),
            pltpu.VMEM((4, 128, 256), F32),
            pltpu.VMEM((4, 256, 128), F32),
            pltpu.VMEM((levels, 4, 128, 256), F32),
            pltpu.VMEM((levels, 4, 256, 256), BF16),
            pltpu.VMEM((4, 256, 256), BF16),
            pltpu.VMEM((4, 256, 128), BF16),
            pltpu.VMEM((NODES << bits, 1, 256), F32),
            pltpu.VMEM((slots, WIDE, RANK), F32),
            pltpu.VMEM((slots, WIDE, RANK), F32),
            pltpu.VMEM((CHUNKS, WIDE, RANK), F32),
            pltpu.VMEM((6, 4, 128, 128), F32),
            pltpu.VMEM((2, 4, 256, 128), F32),
            pltpu.SemaphoreType.DMA((slots,)),
            pltpu.SemaphoreType.DMA((slots,)),
            pltpu.SemaphoreType.DMA((len(mates),)),
            pltpu.SemaphoreType.DMA((len(mates),)),
            pltpu.SemaphoreType.DMA((levels, 4)),
            pltpu.SemaphoreType.DMA((2, 4)),
            pltpu.SemaphoreType.DMA((4,)),
            pltpu.SemaphoreType.DMA((4,)),
            pltpu.SemaphoreType.DMA((4,)),
            pltpu.SemaphoreType.DMA((2, 4)),
        ],
        compiler_params=pltpu.CompilerParams(
            collective_id=0, has_side_effects=True, vmem_limit_bytes=60 << 20
        ),
        name="butterfly",
    )(block_index, source, leaf_in, factors, leaf_out, weight_table)


def solution(mesh):
    placed = (
        P(("row", "col"), None),
        P(("row", "col"), None, None),
        P(None, ("row", "col"), None, None),
        P(("row", "col"), None, None),
        P(("row", "col"), None),
        P(("row", "col")),
    )
    return jax.shard_map(
        body, mesh=mesh, in_specs=placed, out_specs=P(("row", "col"), None), check_vma=False
    )
```

time: 800 us -> 134 us (0.17)
  waiting for transfers between devices: 686 us -> 0 us
  Pallas kernels: 0 us -> 130 us
  starting transfers between devices: 48.9 us -> 0 us
  matrix products: 41.8 us -> 0 us
  between operations: 13.9 us -> 0.01 us
    all_gather x1 -> x0, waiting for transfers between devices: 496 us -> none  [body(): piece = lax.all_gather(weight_table, ('row', 'col'), axis=0, tiled=True)]
    ppermute x16 -> x0, waiting for transfers between devices: 190 us -> none  [partner_2(): lax.ppermute(value, axis, [(i, i ^ 1 << bit) for i in range(lax.axis_size...]
    pallas_call x0 -> x1, Pallas kernels: none -> 130 us  [body(): pl.pallas_call(functools.partial(kernel, levels, col_bits), out_shape=jax...]
    ppermute x16 -> x0, starting transfers between devices: 48.9 us -> none  [partner_2(): lax.ppermute(value, axis, [(i, i ^ 1 << bit) for i in range(lax.axis_size...]
    dot_general x35 -> x0, matrix products: 41.8 us -> none  [the longest x10 20.2 us: body(): jnp.einsum('nrk,nks->nrs', factors[level_index], stacked, precision=HIGH)]
  transfers between devices with their start and end apart: 17 -> 0, of which waited for: 16 -> 0; matrix products, arithmetic and copies ran while one was open for 2% -> 0% of each run, Pallas kernels for 0% -> 0%
where the time goes in v2:
time: 134 us; the launch traced here: 132 us
  Pallas kernels  130 us (97%)
  local copies, waits for them, and re-layouts  2.26 us (2%)
    pallas_call x1, Pallas kernels, body(): pl.pallas_call(functools.partial(kernel, levels, col_bits), out_shape=jax...  130 us

profile of v2, /device:TPU:1, one launch (start us, length us, event | category | flops | bytes accessed | tf_op | source)
XLA Modules:
  0.0 132.2 jit_solution(6906312423120357873)
XLA Ops:
  0.0 129.9 %butterfly.1 = f32[1024,256]{1,0:T(8,128)} custom-call(s32[4]{0:T(128)} %index_ref.1, f32[1024,256]{1,0:T(8,128)} %source_ref.1, f32[4,128,256]{2,1,0:T(8,128)} %leaf_in_ref.1, f32[10,4,128,256]{3,2,1,0:T(8,128)} %factors_ref.1, f32[4,256,128]{2,1,0:T(8,128)} %leaf_out_ref.1, f32[4,256]{1,0:T(4,128)} %table_ref.1), custom_call_target="tpu_custom_call" | custom-call | tf_op jit(solution)/shard_map/butterfly/pallas_call | solution.py:314
  129.9 2.3 %copy.8 = f32[1024,256]{1,0:T(8,128)} copy(f32[1024,256]{1,0:T(8,128)} %butterfly.1) | data formatting | bytes 2097152

commit v3 on v2

--- a/solution.py
+++ b/solution.py
@@ -16,12 +16,37 @@
 HOP = {2: 5.0, 3: 6.2, 4: 3.0, 5: 3.6, 6: 1.8, 7: 3.2, 8: 3.0, 9: 3.8}
 INTERVAL = 2.6
 SECOND_AT = 9.0
+ORDER = (
+    (0,), (1,), (2,), (272,), (16,), (3,), (17,), (4,), (273,), (18,), (5,), (32,), (19,), (6,),
+    (-1,), (274,), (33,), (48,), (20,), (7,), (34,), (49,), (21,), (8,), (64,), (35,), (50,), (80,),
+    (22,), (9,), (65,), (275,), (36,), (51,), (81,), (23, 96), (10,), (66,), (37,), (52,), (82,),
+    (24, 97), (11,), (67,), (112,), (38,), (53,), (83,), (25, 98), (12,), (68,), (113,), (276,),
+    (39,), (128, 54), (84,), (26, 99), (13,), (69,), (114,), (277,), (40,), (129, 55), (85,), (144,),
+    (27, 100), (14,), (70,), (115,), (278,), (41,), (130, 56), (86,), (145,), (160,), (28, 101),
+    (15,), (71,), (116,), (279,), (42,), (131, 57), (87,), (146,), (161,), (29, 102, 72), (176, 117),
+    (43,), (132, 58), (88,), (147,), (162, 192), (30, 103, 73), (177, 118), (44,), (133, 59), (89,),
+    (148,), (163, 193), (31, 104, 74), (178, 119), (208,), (45,), (134, 60), (90,), (149,),
+    (164, 194), (105, 75), (179, 120), (209,), (46, 224), (135, 61), (91,), (150,), (165, 195),
+    (106, 76), (180, 121), (210,), (47, 225), (136, 62), (92,), (151,), (166, 196), (107, 77),
+    (181, 122), (211,), (226,), (137, 63), (93,), (152,), (167, 240, 197), (108, 78), (182, 123),
+    (212,), (227,), (138,), (94,), (153,), (168, 241, 198), (109, 79), (183, 124), (213,), (228,),
+    (139,), (95,), (154,), (169, 242, 199), (110,), (184, 125), (214,), (229,), (140,), (155,),
+    (170, 243, 200), (111,), (185, 126), (215,), (230,), (141,), (156,), (171, 244, 201), (186, 127),
+    (216,), (231,), (142,), (157,), (172, 245, 202), (187,), (217,), (232,), (143,), (158,),
+    (173, 246, 203), (188,), (218,), (233,), (256,), (159,), (174, 247, 204), (189,), (219,), (234,),
+    (257,), (175, 248, 205), (190,), (220,), (235,), (258,), (249, 206), (191,), (221,), (236,),
+    (259,), (250, 207), (222,), (237,), (260,), (251,), (223,), (238,), (261,), (252,), (239,),
+    (262,), (253,), (263,), (254,), (264,), (255,), (265,), (266,), (267,), (268,), (269,), (270,),
+    (271,),
+)
 GATHER = ((0, 1, 5), (2, 3), (6, 7), (4,))
 GATHER_AT = (0.1, 10.0, 19.0, 31.0)
 GRAM_AT = 38.0
 
 
 def plan(levels):
+    if levels == 10:
+        return ORDER
     order = list(range(2, levels)) + list(range(levels - 1, 1, -1))
     at = [0.0]
     for level in order:
@@ -36,7 +61,7 @@
         events.append((min(GATHER_AT[k], gram_at - 0.1 + 0.01 * k), 1, base + k))
     for n in range(NODES):
         events.append((gram_at + n * INTERVAL, 1, base + rounds + n))
-    return [code for _, _, code in sorted(events)]
+    return [(code,) for _, _, code in sorted(events)]
 
 
 def gather_rounds(bits):
@@ -95,15 +120,14 @@
 def kernel(
     levels, col_bits,
     index_ref, source_ref, leaf_in_ref, factors_ref, leaf_out_ref, table_ref, result_ref,
-    src_v, lin_v, lout_v, fac_v, fb_v, linb_v, gram_v, tab_v, send_v, recv_v, own_v, loc_v, out_v,
-    send_sem, recv_sem, tsend_sem, trecv_sem, fac_sem, src_sem, lin_sem, lout_sem, tab_sem, out_sem,
+    src_v, lin_v, lout_v, fac_v, fb_v, linb_v, gram_v, tab_v, send_v, recv_v, own_v, loc_v,
+    send_sem, recv_sem, tsend_sem, trecv_sem, fac_sem, src_sem, lin_sem, lout_sem, tab_sem,
 ):
     bits = levels - 2
     cols = 1 << col_bits
     row, col = lax.axis_index("row"), lax.axis_index("col")
     device = row * cols + col
     exchanges = 2 * bits
-    events = plan(levels)
     gather_bits = [b for group in GATHER for b in group if b < bits]
     rounds = gather_rounds(bits)
 
@@ -152,6 +176,7 @@
             load_factor(level, n).start()
     for n in range(NODES):
         load_table(n).start()
+        load_source(1, n).start()
 
     def exchange(e, slot):
         b = e if e < bits else exchanges - 1 - e
@@ -183,10 +208,6 @@
     def split_factor(level, n):
         load_factor(level, n).wait()
         fb_v[level, n] = stacked(fac_v[level, n])
-
-    def store(h, q):
-        lanes = pl.ds(h * 128, 128)
-        return pltpu.make_async_copy(out_v.at[h, q], result_ref.at[pl.ds(q * 256, 256), lanes], out_sem.at[h, q])
 
     def start_half(h):
         for n in range(NODES):
@@ -223,8 +244,7 @@
         if n == 3 and rows.stop == 128:
             for m in range(NODES):
                 block = backward(loc_v[4, m] + loc_v[5, m ^ 1], linb_v[m])
-                out_v[h, m] = block.T
-                store(h, m).start()
+                result_ref[m * 256 : (m + 1) * 256, h * 128 : (h + 1) * 128] = block.T
 
     def make_gram(n):
         load_leaf_out(n).wait()
@@ -235,10 +255,7 @@
         gram_v[n] = stacked(gram)
 
     start_half(0)
-    for n in range(NODES):
-        load_factor(2, n).start()
-        load_source(1, n).start()
-    for level in range(3, levels):
+    for level in range(2, levels):
         for n in range(NODES):
             load_factor(level, n).start()
     for n in range(NODES):
@@ -252,7 +269,7 @@
             start_half(1)
             return
         s, c = code // CHUNKS, code % CHUNKS
-        n, before = c % NODES, code - CHUNKS
+        before = code - CHUNKS
         if s > exchanges:
             k = code - (exchanges + 1) * CHUNKS
             if 0 < k <= len(rounds):
@@ -263,33 +280,50 @@
                     copy.start()
             else:
                 make_gram(k - len(rounds))
-            return
-        if s > 0:
+        elif s == 0:
+            exchange(0, code).start()
+            after(code)
+        else:
             exchange(s - 1, before).wait_recv()
-        if s < bits and s > 0:
-            both = jnp.concatenate([send_v[before], recv_v[before]], axis=1)
-            send_v[code] = forward(both, fb_v[s + 1, n])
-        elif s == bits:
-            both = jnp.concatenate([send_v[before], recv_v[before]], axis=1)
-            new = forward(both, fb_v[levels - 1, n])
-            both = backward(backward(new, gram_v[n]), fb_v[levels - 1, n])
-            own_v[c] = both[:, :RANK]
-            send_v[code] = both[:, RANK:]
-        elif s > bits and s < exchanges:
-            both = backward(own_v[c] + recv_v[before], fb_v[exchanges + 1 - s, n])
-            own_v[c] = both[:, :RANK]
-            send_v[code] = both[:, RANK:]
-        if s < exchanges:
+            finish(c, own_v[c] + recv_v[before])
+            after(code)
+
+    def compute(code):
+        s, c = code // CHUNKS, code % CHUNKS
+        n, before = c % NODES, code - CHUNKS
+        if 0 < s <= bits:
+            new = forward(jnp.concatenate([send_v[before], recv_v[before]], axis=1), fb_v[s + 1, n])
+            if s < bits:
+                return new
+            return backward(backward(new, gram_v[n]), fb_v[levels - 1, n])
+        return backward(own_v[c] + recv_v[before], fb_v[exchanges + 1 - s, n])
+
+    def run(group):
+        for code in group:
+            exchange(code // CHUNKS - 1, code - CHUNKS).wait_recv()
+        results = [compute(code) for code in group]
+        for code, new in zip(group, results):
+            s, c = code // CHUNKS, code % CHUNKS
+            if s >= bits:
+                own_v[c] = new[:, :RANK]
+                new = new[:, RANK:]
+            send_v[code] = new
             exchange(s, code).start()
+        for code in group:
+            after(code)
+
+    def after(code):
+        s, c = code // CHUNKS, code % CHUNKS
+        if s < bits and c < NODES:
+            split_factor(s + 2, c % NODES)
+        if s >= 2:
+            exchange(s - 2, code - 2 * CHUNKS).wait_send()
+
+    for group in plan(levels):
+        if len(group) > 1 or CHUNKS <= group[0] < exchanges * CHUNKS:
+            run(group)
         else:
-            finish(c, own_v[c] + recv_v[before])
-        if s < bits and c < NODES:
-            split_factor(s + 2, n)
-        if s >= 2:
-            exchange(s - 2, before - CHUNKS).wait_send()
-
-    for code in events:
-        event(code)
+            event(group[0])
 
     def drain(c, carry):
         exchange(exchanges - 1, (exchanges - 1) * CHUNKS + c).wait_send()
@@ -299,9 +333,6 @@
     for k in range(len(rounds)):
         for copy in gather(k):
             copy.wait_send()
-    for h in range(2):
-        for q in range(NODES):
-            store(h, q).wait()
 
 
 def body(source, leaf_in, factors, leaf_out, weight_table, block_index):
@@ -313,9 +344,9 @@
     anywhere = pl.BlockSpec(memory_space=pl.ANY)
     return pl.pallas_call(
         functools.partial(kernel, levels, col_bits),
-        out_shape=jax.ShapeDtypeStruct(source.shape, F32),
+        out_shape=pltpu.VMEM(source.shape, F32),
         in_specs=[pl.BlockSpec(memory_space=pltpu.SMEM)] + [anywhere] * 5,
-        out_specs=anywhere,
+        out_specs=pl.BlockSpec(memory_space=pltpu.VMEM),
         scratch_shapes=[
             pltpu.VMEM((2, 4, 256, 128), F32),
             pltpu.VMEM((4, 128, 256), F32),
@@ -329,7 +360,6 @@
             pltpu.VMEM((slots, WIDE, RANK), F32),
             pltpu.VMEM((CHUNKS, WIDE, RANK), F32),
             pltpu.VMEM((6, 4, 128, 128), F32),
-            pltpu.VMEM((2, 4, 256, 128), F32),
             pltpu.SemaphoreType.DMA((slots,)),
             pltpu.SemaphoreType.DMA((slots,)),
             pltpu.SemaphoreType.DMA((len(mates),)),
@@ -339,7 +369,6 @@
             pltpu.SemaphoreType.DMA((4,)),
             pltpu.SemaphoreType.DMA((4,)),
             pltpu.SemaphoreType.DMA((4,)),
-            pltpu.SemaphoreType.DMA((2, 4)),
         ],
         compiler_params=pltpu.CompilerParams(
             collective_id=0, has_side_effects=True, vmem_limit_bytes=60 << 20

time: 134 us -> 128 us (0.955); the launches traced: 132 us -> 128 us
  Pallas kernels: 130 us -> 127 us
    pallas_call x1, Pallas kernels: 130 us -> 127 us  [body(): pl.pallas_call(functools.partial(kernel, levels, col_bits), out_shape=plt...]
where the time goes in v3:
time: 128 us
  Pallas kernels  127 us (99%)
    pallas_call x1, Pallas kernels, body(): pl.pallas_call(functools.partial(kernel, levels, col_bits), out_shape=plt...  127 us

profile of v3, /device:TPU:1, one launch (start us, length us, event | category | flops | bytes accessed | tf_op | source)
XLA Modules:
  0.0 128.3 jit_solution(954058080282189697)
XLA Ops:
  0.0 127.3 %butterfly.1 = f32[1024,256]{1,0:T(8,128)S(1)} custom-call(s32[4]{0:T(128)} %index_ref.1, f32[1024,256]{1,0:T(8,128)} %source_ref.1, f32[4,128,256]{2,1,0:T(8,128)} %leaf_in_ref.1, f32[10,4,128,256]{3,2,1,0:T(8,128)} %factors_ref.1, f32[4,256,128]{2,1,0:T(8,128)} %leaf_out_ref.1, f32[4,256]{1,0:T(4,128)} %table_ref.1), custom_call_target="tpu_custom_call" | custom-call | tf_op jit(solution)/shard_map/butterfly/pallas_call | solution.py:345
  127.3 1.0 copy.8

commit v4 on v3

--- a/solution.py
+++ b/solution.py
@@ -17,27 +17,27 @@
 INTERVAL = 2.6
 SECOND_AT = 9.0
 ORDER = (
-    (0,), (1,), (2,), (272,), (16,), (3,), (17,), (4,), (273,), (18,), (5,), (32,), (19,), (6,),
-    (-1,), (274,), (33,), (48,), (20,), (7,), (34,), (49,), (21,), (8,), (64,), (35,), (50,), (80,),
-    (22,), (9,), (65,), (275,), (36,), (51,), (81,), (23, 96), (10,), (66,), (37,), (52,), (82,),
-    (24, 97), (11,), (67,), (112,), (38,), (53,), (83,), (25, 98), (12,), (68,), (113,), (276,),
-    (39,), (128, 54), (84,), (26, 99), (13,), (69,), (114,), (277,), (40,), (129, 55), (85,), (144,),
-    (27, 100), (14,), (70,), (115,), (278,), (41,), (130, 56), (86,), (145,), (160,), (28, 101),
-    (15,), (71,), (116,), (279,), (42,), (131, 57), (87,), (146,), (161,), (29, 102, 72), (176, 117),
-    (43,), (132, 58), (88,), (147,), (162, 192), (30, 103, 73), (177, 118), (44,), (133, 59), (89,),
-    (148,), (163, 193), (31, 104, 74), (178, 119), (208,), (45,), (134, 60), (90,), (149,),
-    (164, 194), (105, 75), (179, 120), (209,), (46, 224), (135, 61), (91,), (150,), (165, 195),
-    (106, 76), (180, 121), (210,), (47, 225), (136, 62), (92,), (151,), (166, 196), (107, 77),
-    (181, 122), (211,), (226,), (137, 63), (93,), (152,), (167, 240, 197), (108, 78), (182, 123),
-    (212,), (227,), (138,), (94,), (153,), (168, 241, 198), (109, 79), (183, 124), (213,), (228,),
-    (139,), (95,), (154,), (169, 242, 199), (110,), (184, 125), (214,), (229,), (140,), (155,),
-    (170, 243, 200), (111,), (185, 126), (215,), (230,), (141,), (156,), (171, 244, 201), (186, 127),
-    (216,), (231,), (142,), (157,), (172, 245, 202), (187,), (217,), (232,), (143,), (158,),
-    (173, 246, 203), (188,), (218,), (233,), (256,), (159,), (174, 247, 204), (189,), (219,), (234,),
-    (257,), (175, 248, 205), (190,), (220,), (235,), (258,), (249, 206), (191,), (221,), (236,),
-    (259,), (250, 207), (222,), (237,), (260,), (251,), (223,), (238,), (261,), (252,), (239,),
-    (262,), (253,), (263,), (254,), (264,), (255,), (265,), (266,), (267,), (268,), (269,), (270,),
-    (271,),
+    (0,), (272,), (1,), (2,), (16,), (3,), (17,), (4,), (273,), (-1,), (18,), (5,), (32,), (19,),
+    (6,), (33,), (48,), (274,), (20,), (7,), (34,), (49,), (21,), (8,), (64,), (35,), (50,), (80,),
+    (22,), (9,), (65,), (36,), (51,), (81,), (23,), (66,), (10,), (96,), (37,), (275,), (52,), (82,),
+    (24,), (67, 97), (11,), (112,), (38,), (53,), (83,), (25, 68), (98,), (12,), (113,), (276,),
+    (39,), (128,), (54,), (84,), (69, 26, 99), (13,), (114,), (277,), (40,), (129,), (55,), (85,),
+    (144,), (70, 100, 27), (14,), (115,), (278,), (41,), (130,), (56,), (86,), (145,), (71, 101),
+    (160, 28), (15,), (116,), (279,), (42,), (131,), (57,), (87,), (146,), (72, 102), (161, 29),
+    (117, 176), (43,), (132,), (58, 88), (192, 147), (73, 103, 162), (30,), (118, 177), (44,),
+    (133,), (59, 89), (193, 148), (104, 74, 163), (31, 208), (119, 178), (45,), (134,), (60, 90),
+    (194, 149), (164, 105, 75), (209, 224), (120, 179), (46,), (135,), (61, 91), (195, 150),
+    (165, 106), (76,), (210, 225), (121, 180), (47,), (136,), (62, 92), (196, 151), (166,),
+    (107, 77), (211, 226), (181, 122), (240,), (137,), (63, 93), (197, 152), (167,), (108, 78, 212),
+    (227,), (182,), (123,), (241,), (138,), (94,), (198,), (153,), (168,), (109, 213, 79), (228,),
+    (183,), (124,), (242,), (139,), (95,), (199,), (154,), (169,), (214, 110, 229), (184,), (125,),
+    (243,), (140,), (200,), (155,), (170,), (215, 230), (111,), (185,), (126,), (244,), (141,),
+    (201,), (156,), (171, 216), (231,), (186,), (127,), (245,), (142,), (202,), (157,), (172, 217),
+    (232,), (187,), (246,), (143,), (203,), (158,), (173, 218), (233,), (188,), (247,), (204,),
+    (159,), (174, 219), (234,), (189,), (248,), (205,), (175,), (256,), (220, 235), (190,), (249,),
+    (206,), (257,), (221, 236), (191,), (250,), (207,), (258,), (222, 237), (251,), (259,),
+    (223, 238), (252,), (260,), (239,), (253,), (261,), (254,), (262,), (255,), (263,), (264,),
+    (265,), (266,), (267,), (268,), (269,), (270,), (271,),
 )
 GATHER = ((0, 1, 5), (2, 3), (6, 7), (4,))
 GATHER_AT = (0.1, 10.0, 19.0, 31.0)

time: 128 us -> 127 us (level)
  no operation moved by 1% of the time
where the time goes in v4:
time: 127 us
  Pallas kernels  126 us (99%)
    pallas_call x1, Pallas kernels, body(): pl.pallas_call(functools.partial(kernel, levels, col_bits), out_shape=plt...  126 us

profile of v4, /device:TPU:1, one launch (start us, length us, event | category | flops | bytes accessed | tf_op | source)
XLA Modules:
  0.0 127.0 jit_solution(7590943965182145473)
XLA Ops:
  0.0 126.0 %butterfly.1 = f32[1024,256]{1,0:T(8,128)S(1)} custom-call(s32[4]{0:T(128)} %index_ref.1, f32[1024,256]{1,0:T(8,128)} %source_ref.1, f32[4,128,256]{2,1,0:T(8,128)} %leaf_in_ref.1, f32[10,4,128,256]{3,2,1,0:T(8,128)} %factors_ref.1, f32[4,256,128]{2,1,0:T(8,128)} %leaf_out_ref.1, f32[4,256]{1,0:T(4,128)} %table_ref.1), custom_call_target="tpu_custom_call" | custom-call | tf_op jit(solution)/shard_map/butterfly/pallas_call | solution.py:345
  126.0 1.0 copy.8
